TPU v7x, 256 devices: a whole 4x4x8 slice. The times are simulated.
256 devices in a mesh: alpha: 16 (over y, x_hi, core), beta: 16 (over x_lo, z).
Axes of the slice: x: 4 (x_hi: 2, x_lo: 2; x = x_hi * 2 + x_lo), y: 4, z: 8, core: 2. Of those that a mesh axis runs over, the one named last changes fastest.
Arguments:
- coefficients: float32 [12288, 12288], P('alpha', 'beta'), may hold values from -6 to 6
- beta_blocks: float32 [32, 3, 384, 384], P('beta'), may hold values from -0.1875 to 0.1875
- alpha_blocks: float32 [32, 3, 384, 384], P('alpha'), may hold values from -0.1875 to 0.1875
- beta_links: int32 [32, 3], P('beta'), may hold values from 0 to 31, as said below
- alpha_links: int32 [32, 3], P('alpha'), may hold values from 0 to 31, as said below
- beta_count: int32 [32], P('beta'), may hold values from 1 to 3, as said below
- alpha_count: int32 [32], P('alpha'), may hold values from 1 to 3, as said below
Outputs:
- sigma_slab: float32 [12288, 12288], P('alpha', 'beta')
Inputs may be any that keep to these rules, and one draw needn't show every extreme that they name: `beta_links`: each row lists 3 distinct beta groups whose cyclic distance from the row's own group is at most 2. `alpha_links`: each row lists 3 distinct alpha groups whose cyclic distance from the row's own group is at most 2. `beta_count`: some group uses all 3 couplings. `alpha_count`: some group uses all 3 couplings.
All inputs are finite; a program needn't handle non-finite values.
Results may differ from a plain program's by a relative error of at most 0.0003.
Values sent between devices are 32-bit elements; how exact they have to be, the bound alone decides.
A program may use at most 128 MiB of HBM per device.

v0:
```python
import functools

import jax
import jax.numpy as jnp
from jax import lax
from jax.experimental import pallas as pl
from jax.experimental.pallas import tpu as pltpu
from jax.sharding import PartitionSpec as P

MESH = pl.DeviceIdType.MESH
G = 384
GPD = 2
LIST = 3
S = G * GPD
CHUNKS = 24
R = S // CHUNKS


def split(x):
    high = x.astype(jnp.bfloat16)
    return high, (x - high.astype(jnp.float32)).astype(jnp.bfloat16)


def product(a_high, a_low, b_high, b_low):
    dot = functools.partial(jnp.dot, preferred_element_type=jnp.float32)
    return dot(a_high, b_high) + dot(a_low, b_high) + dot(a_high, b_low)


def kernel(
    na, nb,
    c_ref, hb_ref, ha_ref, lb_ref, la_ref, cb_ref, ca_ref,
    out_ref,
    own, near, far, left, right, relay, hb, ha,
    own_h, own_l, near_h, near_l, kb_h, kb_l, ka_h, ka_l,
    send_sem, recv_sem, near_send, near_recv, local_sem,
):
    a, b = lax.axis_index("alpha"), lax.axis_index("beta")
    nz = nb // 2
    core, z = lax.rem(a, 2), lax.rem(b, nz)
    column = b - z
    core_device = (a + 1 - 2 * core, b)
    inner_device = (a, lax.rem(b + nz, nb))
    outer_device = (lax.rem(a + 2 * core + na - 1, na), lax.rem(b + nz, nb))
    up_device = (a, column + lax.rem(z + 1, nz))
    down_device = (a, column + lax.rem(z + nz - 1, nz))

    own_copy = pltpu.make_async_copy(c_ref, own, local_sem.at[0])
    hb_copy = pltpu.make_async_copy(hb_ref, hb, local_sem.at[1])
    ha_copy = pltpu.make_async_copy(ha_ref, ha, local_sem.at[2])
    own_copy.start()
    hb_copy.start()
    ha_copy.start()

    barrier = pltpu.get_barrier_semaphore()
    for device in (core_device, inner_device, outer_device, up_device, down_device):
        pl.semaphore_signal(barrier, inc=1, device_id=device, device_id_type=MESH)
    pl.semaphore_wait(barrier, 5)

    def remote(source, target, flow, k, device):
        rows = pl.ds(k * R, R)
        return pltpu.make_async_remote_copy(
            src_ref=source.at[rows],
            dst_ref=target.at[rows],
            send_sem=send_sem.at[flow, k],
            recv_sem=recv_sem.at[flow, k],
            device_id=device,
            device_id_type=MESH,
        )

    def to_inner(k):
        return remote(c_ref, relay, 0, k, inner_device)

    def to_outer(k):
        return remote(relay, far, 1, k, outer_device)

    def to_up(k, source=c_ref):
        return remote(source, left, 2, k, up_device)

    def to_down(k, source=c_ref):
        return remote(source, right, 3, k, down_device)

    to_core = pltpu.make_async_remote_copy(
        src_ref=c_ref, dst_ref=near, send_sem=near_send, recv_sem=near_recv,
        device_id=core_device, device_id_type=MESH,
    )

    @pl.loop(0, CHUNKS)
    def _(k):
        to_inner(k).start()

        @pl.when(z != nz - 1)
        def _():
            to_up(k).start()

        @pl.when(z != 0)
        def _():
            to_down(k).start()

    to_core.start()

    def forward(k):
        to_inner(k).wait_recv()
        to_outer(k).start()

        @pl.when(z == nz - 1)
        def _():
            to_up(k, relay).start()

        @pl.when(z == 0)
        def _():
            to_down(k, relay).start()

    def select(blocks, links, counts, t, group, rows):
        total = None
        for l in range(LIST):
            used = jnp.logical_and(links[t, l] == group, l < counts[t])
            term = jnp.where(used, 1.0, 0.0) * blocks[t, l, rows, :]
            total = term if total is None else total + term
        return total

    def build(s):
        for t in range(GPD):
            beta_group = lax.rem(GPD * (b + nb - 1) + s, GPD * nb)
            alpha_group = lax.rem(GPD * (a + na - 1) + s, GPD * na)
            at = pl.multiple_of(s * G, 128)

            @pl.loop(0, G // 64)
            def _(i):
                rows = pl.ds(pl.multiple_of(i * 64, 64), 64)
                high, low = split(select(hb, lb_ref, cb_ref, t, beta_group, rows))
                to = (pl.ds(pl.multiple_of(at + i * 64, 64), 64), pl.ds(t * G, G))
                kb_h[to], kb_l[to] = high, low
                high, low = split(select(ha, la_ref, ca_ref, t, alpha_group, rows))
                to = (pl.ds(pl.multiple_of(t * G + i * 64, 64), 64), pl.ds(at, G))
                ka_h[to], ka_l[to] = high, low

        rows = pl.ds(pl.multiple_of(s * 128, 128), 128)
        own_h[rows, :], own_l[rows, :] = split(own[rows, :])

    near_at = jnp.where(core == 1, 0, 2 * S)
    far_at = 2 * S - near_at

    own_copy.wait()
    hb_copy.wait()
    ha_copy.wait()

    @pl.loop(0, 6)
    def _(s):
        forward(s)
        build(s)

    to_core.wait_recv()

    @pl.loop(0, 3)
    def _(i):
        forward(6 + i)
        rows = pl.ds(pl.multiple_of(i * 256, 256), 256)
        mine = pl.ds(S, S)
        near_h[rows, :], near_l[rows, :] = split(near[rows, :])
        out_ref[rows, :] = product(own_h[rows, :], own_l[rows, :], kb_h[mine, :], kb_l[mine, :])
        out_ref[rows, :] += product(ka_h[rows, mine], ka_l[rows, mine], own_h[...], own_l[...])

    @pl.loop(0, 3)
    def _(i):
        forward(9 + i)
        rows = pl.ds(pl.multiple_of(i * 256, 256), 256)
        mine = pl.ds(pl.multiple_of(near_at, 256), S)
        out_ref[rows, :] += product(ka_h[rows, mine], ka_l[rows, mine], near_h[...], near_l[...])

    def sides(j):
        rows = pl.ds(pl.multiple_of(j * 128, 128), 128)

        @pl.loop(4 * j, 4 * j + 4)
        def _(k):
            to_up(k).wait_recv()
            to_down(k).wait_recv()

        for part, at in ((left, 0), (right, 2 * S)):
            mine = pl.ds(at, S)
            out_ref[rows, :] += product(*split(part[rows, :]), kb_h[mine, :], kb_l[mine, :])

    def outer(j):
        rows = pl.ds(pl.multiple_of(j * 128, 128), 128)
        mine = pl.ds(pl.multiple_of(far_at + j * 128, 128), 128)

        @pl.loop(4 * j, 4 * j + 4)
        def _(k):
            to_outer(k).wait_recv()

        high, low = split(far[rows, :])

        @pl.loop(0, 3)
        def _(i):
            block = pl.ds(pl.multiple_of(i * 256, 256), 256)
            out_ref[block, :] += product(ka_h[block, mine], ka_l[block, mine], high, low)

    @pl.loop(0, 4)
    def _(j):
        forward(12 + 2 * j)
        sides(j)
        forward(13 + 2 * j)
        outer(j)

    @pl.loop(20, CHUNKS)
    def _(k):
        forward(k)

    @pl.loop(4, 6)
    def _(j):
        sides(j)
        outer(j)

    to_core.wait_send()

    @pl.loop(0, CHUNKS)
    def _(k):
        to_inner(k).wait_send()
        to_outer(k).wait_send()
        to_up(k).wait_send()
        to_down(k).wait_send()


def solution(mesh):
    na, nb = mesh.shape["alpha"], mesh.shape["beta"]

    def on_device(
        coefficients, beta_blocks, alpha_blocks, beta_links, alpha_links, beta_count, alpha_count
    ):
        block = pltpu.VMEM((S, S), jnp.float32)
        listed = pltpu.VMEM((GPD, LIST, G, G), jnp.float32)
        half = pltpu.VMEM((S, S), jnp.bfloat16)
        tall = pltpu.VMEM((3 * S, S), jnp.bfloat16)
        wide = pltpu.VMEM((S, 3 * S), jnp.bfloat16)
        return pl.pallas_call(
            functools.partial(kernel, na, nb),
            out_shape=jax.ShapeDtypeStruct((S, S), jnp.float32),
            in_specs=[pl.BlockSpec(memory_space=pl.ANY)] * 3
            + [pl.BlockSpec(memory_space=pltpu.SMEM)] * 4,
            out_specs=pl.BlockSpec(memory_space=pltpu.VMEM),
            scratch_shapes=[block] * 6
            + [listed] * 2
            + [half] * 4
            + [tall, tall, wide, wide]
            + [
                pltpu.SemaphoreType.DMA((4, CHUNKS)),
                pltpu.SemaphoreType.DMA((4, CHUNKS)),
                pltpu.SemaphoreType.DMA(()),
                pltpu.SemaphoreType.DMA(()),
                pltpu.SemaphoreType.DMA((3,)),
            ],
            compiler_params=pltpu.CompilerParams(
                collective_id=0, has_side_effects=True, vmem_limit_bytes=58 * 2**20
            ),
            name="sigma",
        )(
            coefficients, beta_blocks, alpha_blocks,
            beta_links, alpha_links, beta_count, alpha_count,
        )

    return jax.shard_map(
        on_device,
        mesh=mesh,
        in_specs=(
            P("alpha", "beta"),
            P("beta", None, None, None),
            P("alpha", None, None, None),
            P("beta", None),
            P("alpha", None),
            P("beta"),
            P("alpha"),
        ),
        out_specs=P("alpha", "beta"),
        check_vma=False,
    )
```

profile of v0, /device:TPU:2, one launch (start us, length us, event | category | flops | bytes accessed | tf_op | source)
XLA Modules:
  0.0 73.8 jit_solution(7799081300136382982)
XLA Ops:
  0.0 70.6 %sigma.1 = f32[768,768]{1,0:T(8,128)} custom-call(f32[768,768]{1,0:T(8,128)} %c_ref.1, f32[2,3,384,384]{3,2,1,0:T(8,128)} %hb_ref.1, f32[2,3,384,384]{3,2,1,0:T(8,128)} %ha_ref.1, s32[2,3]{1,0:T(2,128)} %lb_ref.1, s32[2,3]{1,0:T(2,128)} %la_ref.1, s32[2]{0:T(128)} %cb_ref.1, s32[2]{0:T(128)} %ca_ref.1), custom_call_target="tpu_custom_call" | custom-call | tf_op jit(solution)/shard_map/sigma/pallas_call | solution.py:234
  70.6 3.2 %copy.9 = f32[768,768]{1,0:T(8,128)} copy(f32[768,768]{1,0:T(8,128)} %sigma.1) | data formatting | bytes 4718592
where the time goes:
time: 74.1 us; the launch traced here: 73.8 us
  Pallas kernels  70.6 us (95%)
  local copies, waits for them, and re-layouts  3.22 us (4%)
    pallas_call x1, Pallas kernels, on_device(): pl.pallas_call(functools.partial(kernel, na, nb), out_shape=jax.ShapeDtyp...  70.6 us
    unnamed x1, local copies, waits for them, and re-layouts  3.22 us

commit v1 on v0

--- a/solution.py
+++ b/solution.py
@@ -14,6 +14,7 @@
 S = G * GPD
 CHUNKS = 24
 R = S // CHUNKS
+TAIL = 64
 
 
 def split(x):
@@ -31,7 +32,7 @@
     c_ref, hb_ref, ha_ref, lb_ref, la_ref, cb_ref, ca_ref,
     out_ref,
     own, near, far, left, right, relay, hb, ha,
-    own_h, own_l, near_h, near_l, kb_h, kb_l, ka_h, ka_l,
+    own_h, own_l, near_h, near_l, kb_h, kb_l, ka_h, ka_l, tail,
     send_sem, recv_sem, near_send, near_recv, local_sem,
 ):
     a, b = lax.axis_index("alpha"), lax.axis_index("beta")
@@ -137,6 +138,57 @@
         rows = pl.ds(pl.multiple_of(s * 128, 128), 128)
         own_h[rows, :], own_l[rows, :] = split(own[rows, :])
 
+    def arrived(first, size, *copies):
+        @pl.loop(first // R, (first + size) // R)
+        def _(k):
+            for copy in copies:
+                copy(k).wait_recv()
+
+    def sides(first, size):
+        rows = pl.ds(first, size)
+        arrived(first, size, to_up, to_down)
+        for block, at in ((left, 0), (right, 2 * S)):
+            theirs = pl.ds(at, S)
+            out_ref[rows, :] += product(*split(block[rows, :]), kb_h[theirs, :], kb_l[theirs, :])
+
+    def outer(j):
+        rows = pl.ds(pl.multiple_of(j * 128, 128), 128)
+        theirs = pl.ds(pl.multiple_of(far_at + j * 128, 128), 128)
+        arrived(j * 128, 128, to_outer)
+        high, low = split(far[rows, :])
+
+        @pl.loop(0, 3)
+        def _(i):
+            block = pl.ds(pl.multiple_of(i * 256, 256), 256)
+            out_ref[block, :] += product(ka_h[block, theirs], ka_l[block, theirs], high, low)
+
+    def pack_tail(i):
+        theirs = pl.ds(pl.multiple_of(far_at + S - 2 * TAIL, 128), 2 * TAIL)
+
+        @pl.loop(0, 4)
+        def _(step):
+            rows = pl.ds(pl.multiple_of(i * 256 + step * 64, 64), 64)
+            high = ka_h[rows, theirs].astype(jnp.float32)
+            low = ka_l[rows, theirs].astype(jnp.float32)
+            other_high, other_low = pltpu.roll(high, TAIL, 1), pltpu.roll(low, TAIL, 1)
+            first = lax.broadcasted_iota(jnp.int32, high.shape, 1) < TAIL
+            for part, left_half, right_half in ((0, high, other_low), (1, other_high, low)):
+                tail[part, rows, : 2 * TAIL] = jnp.where(first, left_half, right_half).astype(jnp.bfloat16)
+                tail[part, rows, 2 * TAIL :] = jnp.where(first, left_half, 0.0).astype(jnp.bfloat16)
+
+    def outer_tail(part):
+        first = S - TAIL * (2 - part)
+        arrived(first, TAIL, to_outer)
+        high, low = split(far[pl.ds(first, TAIL), :])
+        stacked = jnp.concatenate([high, high, low, jnp.zeros_like(low)], axis=0)
+
+        @pl.loop(0, 3)
+        def _(i):
+            block = pl.ds(pl.multiple_of(i * 256, 256), 256)
+            out_ref[block, :] += jnp.dot(
+                tail[part, block, :], stacked, preferred_element_type=jnp.float32
+            )
+
     near_at = jnp.where(core == 1, 0, 2 * S)
     far_at = 2 * S - near_at
 
@@ -150,74 +202,60 @@
         build(s)
 
     to_core.wait_recv()
+    mine = pl.ds(S, S)
 
     @pl.loop(0, 3)
     def _(i):
         forward(6 + i)
         rows = pl.ds(pl.multiple_of(i * 256, 256), 256)
-        mine = pl.ds(S, S)
-        near_h[rows, :], near_l[rows, :] = split(near[rows, :])
         out_ref[rows, :] = product(own_h[rows, :], own_l[rows, :], kb_h[mine, :], kb_l[mine, :])
-        out_ref[rows, :] += product(ka_h[rows, mine], ka_l[rows, mine], own_h[...], own_l[...])
 
     @pl.loop(0, 3)
     def _(i):
         forward(9 + i)
         rows = pl.ds(pl.multiple_of(i * 256, 256), 256)
-        mine = pl.ds(pl.multiple_of(near_at, 256), S)
-        out_ref[rows, :] += product(ka_h[rows, mine], ka_l[rows, mine], near_h[...], near_l[...])
-
-    def sides(j):
-        rows = pl.ds(pl.multiple_of(j * 128, 128), 128)
-
-        @pl.loop(4 * j, 4 * j + 4)
-        def _(k):
-            to_up(k).wait_recv()
-            to_down(k).wait_recv()
-
-        for part, at in ((left, 0), (right, 2 * S)):
-            mine = pl.ds(at, S)
-            out_ref[rows, :] += product(*split(part[rows, :]), kb_h[mine, :], kb_l[mine, :])
-
-    def outer(j):
-        rows = pl.ds(pl.multiple_of(j * 128, 128), 128)
-        mine = pl.ds(pl.multiple_of(far_at + j * 128, 128), 128)
-
-        @pl.loop(4 * j, 4 * j + 4)
-        def _(k):
-            to_outer(k).wait_recv()
-
-        high, low = split(far[rows, :])
-
-        @pl.loop(0, 3)
-        def _(i):
-            block = pl.ds(pl.multiple_of(i * 256, 256), 256)
-            out_ref[block, :] += product(ka_h[block, mine], ka_l[block, mine], high, low)
+        near_h[rows, :], near_l[rows, :] = split(near[rows, :])
+        out_ref[rows, :] += product(ka_h[rows, mine], ka_l[rows, mine], own_h[...], own_l[...])
+
+    @pl.loop(0, 3)
+    def _(i):
+        forward(12 + i)
+        rows = pl.ds(pl.multiple_of(i * 256, 256), 256)
+        theirs = pl.ds(pl.multiple_of(near_at, 256), S)
+        out_ref[rows, :] += product(ka_h[rows, theirs], ka_l[rows, theirs], near_h[...], near_l[...])
+        pack_tail(i)
 
     @pl.loop(0, 4)
     def _(j):
-        forward(12 + 2 * j)
-        sides(j)
-        forward(13 + 2 * j)
+        forward(15 + 2 * j)
+        sides(pl.multiple_of(j * 128, 128), 128)
+        forward(16 + 2 * j)
         outer(j)
 
-    @pl.loop(20, CHUNKS)
-    def _(k):
-        forward(k)
-
-    @pl.loop(4, 6)
-    def _(j):
-        sides(j)
-        outer(j)
-
+    forward(CHUNKS - 1)
+    sides(512, 128)
+    outer(4)
     to_core.wait_send()
 
-    @pl.loop(0, CHUNKS)
-    def _(k):
-        to_inner(k).wait_send()
-        to_outer(k).wait_send()
-        to_up(k).wait_send()
-        to_down(k).wait_send()
+    def wait_sends(first, last):
+        @pl.loop(first, last)
+        def _(k):
+            to_inner(k).wait_send()
+            to_outer(k).wait_send()
+            to_up(k).wait_send()
+            to_down(k).wait_send()
+
+    wait_sends(0, CHUNKS - 4)
+    for part in range(2):
+        sides(S - TAIL * (2 - part), TAIL)
+        outer_tail(part)
+    wait_sends(CHUNKS - 4, CHUNKS)
+
+
+def store(total_ref, out_ref, sem):
+    copy = pltpu.make_async_copy(total_ref, out_ref, sem)
+    copy.start()
+    copy.wait()
 
 
 def solution(mesh):
@@ -231,16 +269,16 @@
         half = pltpu.VMEM((S, S), jnp.bfloat16)
         tall = pltpu.VMEM((3 * S, S), jnp.bfloat16)
         wide = pltpu.VMEM((S, 3 * S), jnp.bfloat16)
-        return pl.pallas_call(
+        total = pl.pallas_call(
             functools.partial(kernel, na, nb),
-            out_shape=jax.ShapeDtypeStruct((S, S), jnp.float32),
-            in_specs=[pl.BlockSpec(memory_space=pl.ANY)] * 3
+            out_shape=pltpu.VMEM((S, S), jnp.float32),
+            in_specs=[pl.BlockSpec(memory_space=pltpu.HBM)] * 3
             + [pl.BlockSpec(memory_space=pltpu.SMEM)] * 4,
             out_specs=pl.BlockSpec(memory_space=pltpu.VMEM),
             scratch_shapes=[block] * 6
             + [listed] * 2
             + [half] * 4
-            + [tall, tall, wide, wide]
+            + [tall, tall, wide, wide, pltpu.VMEM((2, S, 4 * TAIL), jnp.bfloat16)]
             + [
                 pltpu.SemaphoreType.DMA((4, CHUNKS)),
                 pltpu.SemaphoreType.DMA((4, CHUNKS)),
@@ -256,6 +294,15 @@
             coefficients, beta_blocks, alpha_blocks,
             beta_links, alpha_links, beta_count, alpha_count,
         )
+        return pl.pallas_call(
+            store,
+            out_shape=jax.ShapeDtypeStruct((S, S), jnp.float32),
+            in_specs=[pl.BlockSpec(memory_space=pltpu.VMEM)],
+            out_specs=pl.BlockSpec(memory_space=pl.ANY),
+            scratch_shapes=[pltpu.SemaphoreType.DMA],
+            compiler_params=pltpu.CompilerParams(vmem_limit_bytes=8 * 2**20),
+            name="store",
+        )(total)
 
     return jax.shard_map(
         on_device,

time: 74.1 us -> 70.2 us (0.947)
  local copies, waits for them, and re-layouts: 3.22 us -> 0 us
    unnamed x1 -> x0, local copies, waits for them, and re-layouts: 3.22 us -> none
    pallas_call x1 -> x2, Pallas kernels: 70.6 us -> 70.1 us  [the longest x1 68.7 us: on_device(): pl.pallas_call(functools.partial(kernel, na, nb), out_shape=pltpu.VMEM((S...]
where the time goes in v1:
time: 70.2 us; the launch traced here: 70.1 us
  Pallas kernels  70.1 us (100%)
    pallas_call x1, Pallas kernels, on_device(): pl.pallas_call(functools.partial(kernel, na, nb), out_shape=pltpu.VMEM((S...  68.7 us
    pallas_call x1, Pallas kernels, on_device(): pl.pallas_call(store, out_shape=jax.ShapeDtypeStruct((S, S), jnp.float32)...  1.42 us

profile of v1, /device:TPU:2, one launch (start us, length us, event | category | flops | bytes accessed | tf_op | source)
XLA Modules:
  0.0 70.1 jit_solution(15239494119003269690)
XLA Ops:
  0.0 68.7 %sigma.1.total_ref = f32[768,768]{1,0:T(8,128)S(1)} custom-call(f32[768,768]{1,0:T(8,128)} %c_ref.1, f32[2,3,384,384]{3,2,1,0:T(8,128)} %hb_ref.1, f32[2,3,384,384]{3,2,1,0:T(8,128)} %ha_ref.1, s32[2,3]{1,0:T(2,128)} %lb_ref.1, s32[2,3]{1,0:T(2,128)} %la_ref.1, s32[2]{0:T(128)} %cb_ref.1, s32[2]{0:T(128)} %ca_ref.1), custom_call_target="tpu_custom_call" | custom-call | tf_op jit(solution)/shard_map/sigma/pallas_call | solution.py:272
  68.7 1.4 %store.1 = f32[768,768]{1,0:T(8,128)} custom-call(f32[768,768]{1,0:T(8,128)S(1)} %sigma.1.total_ref), custom_call_target="tpu_custom_call" | custom-call | tf_op jit(solution)/shard_map/store/pallas_call | solution.py:297

commit v2 on v1

v2 whole, which is shorter than its diff:
```python
import functools

import jax
import jax.numpy as jnp
from jax import lax
from jax.experimental import pallas as pl
from jax.experimental.pallas import tpu as pltpu
from jax.sharding import PartitionSpec as P

MESH = pl.DeviceIdType.MESH
G = 384
GPD = 2
LIST = 3
S = G * GPD
R = 64
EVEN = 10
LAST = 96
CHUNKS = EVEN + 2
FINAL = CHUNKS - 1


def split(x):
    high = x.astype(jnp.bfloat16)
    return high, (x - high.astype(jnp.float32)).astype(jnp.bfloat16)


def product(a_high, a_low, b_high, b_low):
    dot = functools.partial(jnp.dot, preferred_element_type=jnp.float32)
    return dot(a_high, b_high) + dot(a_low, b_high) + dot(a_high, b_low)


def chunk(k):
    if isinstance(k, int) and k >= EVEN:
        return pl.ds(*((EVEN * R, S - EVEN * R - LAST), (S - LAST, LAST))[k - EVEN])
    return pl.ds(k * R, R)


def kernel(
    na, nb,
    c_ref, hb_ref, ha_ref, lb_ref, la_ref, cb_ref, ca_ref,
    out_ref,
    own, near, far, left, right, relay, detour, hb, ha,
    own_h, own_l, near_h, near_l, kb_h, kb_l, ka_h, ka_l,
    send_sem, recv_sem, near_sem, detour_sem, local_sem, ready_sem,
):
    a, b = lax.axis_index("alpha"), lax.axis_index("beta")
    nz = nb // 2
    core, z = lax.rem(a, 2), lax.rem(b, nz)
    column = b - z
    low_wrap, high_wrap = z == 0, z == nz - 1
    wrap = jnp.logical_or(low_wrap, high_wrap)
    even = lax.rem(z, 2) == 0
    far_a, inner_b = lax.rem(a + 2 * core + na - 1, na), lax.rem(b + nz, nb)
    core_device = (a + 1 - 2 * core, b)
    inner_device = (a, inner_b)
    outer_device = (far_a, inner_b)
    far_device = (far_a, b)
    up_device = (a, column + lax.rem(z + 1, nz))
    down_device = (a, column + lax.rem(z + nz - 1, nz))

    own_copy = pltpu.make_async_copy(c_ref, own, local_sem.at[0])
    hb_copy = pltpu.make_async_copy(hb_ref, hb, local_sem.at[1])
    ha_copy = pltpu.make_async_copy(ha_ref, ha, local_sem.at[2])
    own_copy.start()
    hb_copy.start()
    ha_copy.start()

    def remote(source, target, flow, k, device):
        return pltpu.make_async_remote_copy(
            src_ref=source.at[chunk(k)],
            dst_ref=target.at[chunk(k)],
            send_sem=send_sem.at[flow, k],
            recv_sem=recv_sem.at[flow, k],
            device_id=device,
            device_id_type=MESH,
        )

    def to_inner(k):
        return remote(c_ref, relay, 0, k, inner_device)

    def to_far(k):
        return remote(c_ref, far, 1, k, far_device)

    def to_outer(k):
        return remote(relay, far, 1, k, outer_device)

    def to_up(k, source=c_ref):
        return remote(source, left, 2, k, up_device)

    def to_down(k, source=c_ref):
        return remote(source, right, 3, k, down_device)

    to_core = pltpu.make_async_remote_copy(
        src_ref=c_ref, dst_ref=near, send_sem=near_sem.at[0], recv_sem=near_sem.at[1],
        device_id=core_device, device_id_type=MESH,
    )
    to_detour = pltpu.make_async_remote_copy(
        src_ref=c_ref.at[chunk(FINAL)], dst_ref=detour,
        send_sem=send_sem.at[2, FINAL], recv_sem=detour_sem.at[0],
        device_id=up_device, device_id_type=MESH,
    )
    from_detour = pltpu.make_async_remote_copy(
        src_ref=detour, dst_ref=left.at[chunk(FINAL)],
        send_sem=detour_sem.at[1], recv_sem=recv_sem.at[2, FINAL],
        device_id=inner_device, device_id_type=MESH,
    )

    def each(body, first=0, last=CHUNKS):
        @pl.loop(first, min(last, EVEN))
        def _(k):
            body(k)

        for k in range(EVEN, last):
            body(k)

    barrier = pltpu.get_barrier_semaphore()
    for device in (core_device, inner_device, outer_device, far_device):
        pl.semaphore_signal(barrier, inc=1, device_id=device, device_id_type=MESH)

    @pl.when(even)
    def _():
        for device in (up_device, down_device):
            pl.semaphore_signal(barrier, inc=1, device_id=device, device_id_type=MESH)

    pl.semaphore_wait(barrier, jnp.where(even, 4, 6))

    @pl.when(jnp.logical_not(even))
    def _():
        for device in (up_device, down_device):
            pl.semaphore_signal(ready_sem, inc=1, device_id=device, device_id_type=MESH)

    @pl.when(wrap)
    def _():
        each(lambda k: to_inner(k).start(), last=FINAL)

    @pl.when(low_wrap)
    def _():
        to_inner(FINAL).start()

    @pl.when(jnp.logical_not(wrap))
    def _():
        each(lambda k: to_far(k).start(), last=FINAL)

    @pl.when(jnp.logical_not(low_wrap))
    def _():
        to_far(FINAL).start()

    @pl.when(even)
    def _():
        pl.semaphore_wait(ready_sem, 2)

    @pl.when(high_wrap)
    def _():
        to_detour.start()

    @pl.when(jnp.logical_not(high_wrap))
    def _():
        each(lambda k: to_up(k).start())

    @pl.when(jnp.logical_not(low_wrap))
    def _():
        each(lambda k: to_down(k).start())

    to_core.start()

    def forward(k):
        @pl.when(wrap)
        def _():
            to_inner(k).wait_recv()

        @pl.when(high_wrap)
        def _():
            to_up(k, relay).start()

        @pl.when(low_wrap)
        def _():
            to_down(k, relay).start()

        @pl.when(wrap)
        def _():
            to_outer(k).start()

    def select(blocks, links, counts, t, group, rows):
        total = None
        for l in range(LIST):
            used = jnp.logical_and(links[t, l] == group, l < counts[t])
            term = jnp.where(used, 1.0, 0.0) * blocks[t, l, rows, :]
            total = term if total is None else total + term
        return total

    def build(s):
        for t in range(GPD):
            beta_group = lax.rem(GPD * (b + nb - 1) + s, GPD * nb)
            alpha_group = lax.rem(GPD * (a + na - 1) + s, GPD * na)
            at = pl.multiple_of(s * G, 128)

            @pl.loop(0, G // 64)
            def _(i):
                rows = pl.ds(pl.multiple_of(i * 64, 64), 64)
                high, low = split(select(hb, lb_ref, cb_ref, t, beta_group, rows))
                to = (pl.ds(pl.multiple_of(at + i * 64, 64), 64), pl.ds(t * G, G))
                kb_h[to], kb_l[to] = high, low
                high, low = split(select(ha, la_ref, ca_ref, t, alpha_group, rows))
                to = (pl.ds(pl.multiple_of(t * G + i * 64, 64), 64), pl.ds(at, G))
                ka_h[to], ka_l[to] = high, low

        rows = pl.ds(pl.multiple_of(s * 128, 128), 128)
        own_h[rows, :], own_l[rows, :] = split(own[rows, :])

    def arrived(copy, first, last):
        @pl.loop(first, min(last, EVEN))
        def _(k):
            copy(k).wait_recv()

        for k in range(max(first, EVEN), last):
            copy(k).wait_recv()

    def side(block, at, first, size):
        rows, theirs = pl.ds(first, size), pl.ds(at, S)
        out_ref[rows, :] += product(*split(block[rows, :]), kb_h[theirs, :], kb_l[theirs, :])

    def sides(first, size):
        for copy, block, at in ((to_up, left, 0), (to_down, right, 2 * S)):
            arrived(copy, first // R, (first + size) // R)
            side(block, at, first, size)

    def outer(first, size):
        theirs = pl.ds(pl.multiple_of(far_at + first, 128), size)
        high, low = split(far[pl.ds(first, size), :])
        stacked = jnp.concatenate([high, high, low], axis=0)

        @pl.loop(0, 3)
        def _(i):
            block = pl.ds(pl.multiple_of(i * 256, 256), 256)
            high, low = ka_h[block, theirs], ka_l[block, theirs]
            wide = jnp.concatenate([high, low, high], axis=1)
            out_ref[block, :] += jnp.dot(wide, stacked, preferred_element_type=jnp.float32)

    near_at = jnp.where(core == 1, 0, 2 * S)
    far_at = 2 * S - near_at
    mine = pl.ds(S, S)

    def third(i):
        return pl.ds(pl.multiple_of(i * 256, 256), 256)

    own_copy.wait()
    hb_copy.wait()
    ha_copy.wait()

    @pl.loop(0, 2)
    def _(step):
        forward(step)

        @pl.loop(0, 3)
        def _(i):
            build(3 * step + i)

    forward(2)

    @pl.loop(0, 3)
    def _(i):
        rows = third(i)
        out_ref[rows, :] = product(own_h[rows, :], own_l[rows, :], kb_h[mine, :], kb_l[mine, :])

    forward(3)

    @pl.loop(0, 3)
    def _(i):
        rows = third(i)
        out_ref[rows, :] += product(ka_h[rows, mine], ka_l[rows, mine], own_h[...], own_l[...])

    forward(4)
    to_core.wait_recv()

    @pl.when(low_wrap)
    def _():
        to_detour.wait_recv()
        from_detour.start()

    @pl.loop(0, 3)
    def _(i):
        rows = third(i)
        near_h[rows, :], near_l[rows, :] = split(near[rows, :])

    forward(5)

    @pl.loop(0, 3)
    def _(i):
        rows = third(i)
        theirs = pl.ds(pl.multiple_of(near_at, 256), S)
        out_ref[rows, :] += product(ka_h[rows, theirs], ka_l[rows, theirs], near_h[...], near_l[...])

    forward(6)
    sides(0, 128)
    forward(7)
    sides(128, 128)
    forward(8)
    arrived(to_far, 0, 4)
    outer(0, 256)
    forward(9)
    sides(256, 128)
    forward(10)
    arrived(to_far, 4, 8)
    outer(256, 256)
    sides(384, 128)

    @pl.when(low_wrap)
    def _():
        forward(FINAL)

    sides(512, 128)
    arrived(to_far, 8, 10)
    outer(512, 128)

    to_core.wait_send()

    @pl.when(wrap)
    def _():
        each(lambda k: to_inner(k).wait_send(), last=FINAL)

    @pl.when(low_wrap)
    def _():
        to_inner(FINAL).wait_send()
        from_detour.wait_send()

    arrived(to_down, EVEN, CHUNKS)
    side(right, 2 * S, 640, 128)
    arrived(to_up, EVEN, CHUNKS)
    side(left, 0, 640, 128)
    arrived(to_far, EVEN, CHUNKS)
    outer(640, 128)

    each(lambda k: to_far(k).wait_send())
    each(lambda k: to_up(k).wait_send())
    each(lambda k: to_down(k).wait_send())


def store(total_ref, out_ref, sem):
    copy = pltpu.make_async_copy(total_ref, out_ref, sem)
    copy.start()
    copy.wait()


def solution(mesh):
    na, nb = mesh.shape["alpha"], mesh.shape["beta"]

    def on_device(
        coefficients, beta_blocks, alpha_blocks, beta_links, alpha_links, beta_count, alpha_count
    ):
        block = pltpu.VMEM((S, S), jnp.float32)
        listed = pltpu.VMEM((GPD, LIST, G, G), jnp.float32)
        half = pltpu.VMEM((S, S), jnp.bfloat16)
        tall = pltpu.VMEM((3 * S, S), jnp.bfloat16)
        wide = pltpu.VMEM((S, 3 * S), jnp.bfloat16)
        total = pl.pallas_call(
            functools.partial(kernel, na, nb),
            out_shape=pltpu.VMEM((S, S), jnp.float32),
            in_specs=[pl.BlockSpec(memory_space=pltpu.HBM)] * 3
            + [pl.BlockSpec(memory_space=pltpu.SMEM)] * 4,
            out_specs=pl.BlockSpec(memory_space=pltpu.VMEM),
            scratch_shapes=[block] * 6
            + [pltpu.VMEM((LAST, S), jnp.float32)]
            + [listed] * 2
            + [half] * 4
            + [tall, tall, wide, wide]
            + [
                pltpu.SemaphoreType.DMA((4, CHUNKS)),
                pltpu.SemaphoreType.DMA((4, CHUNKS)),
                pltpu.SemaphoreType.DMA((2,)),
                pltpu.SemaphoreType.DMA((2,)),
                pltpu.SemaphoreType.DMA((3,)),
                pltpu.SemaphoreType.REGULAR,
            ],
            compiler_params=pltpu.CompilerParams(
                collective_id=0, has_side_effects=True, vmem_limit_bytes=58 * 2**20
            ),
            name="sigma",
        )(
            coefficients, beta_blocks, alpha_blocks,
            beta_links, alpha_links, beta_count, alpha_count,
        )
        return pl.pallas_call(
            store,
            out_shape=jax.ShapeDtypeStruct((S, S), jnp.float32),
            in_specs=[pl.BlockSpec(memory_space=pltpu.VMEM)],
            out_specs=pl.BlockSpec(memory_space=pl.ANY),
            scratch_shapes=[pltpu.SemaphoreType.DMA],
            compiler_params=pltpu.CompilerParams(vmem_limit_bytes=8 * 2**20),
            name="store",
        )(total)

    return jax.shard_map(
        on_device,
        mesh=mesh,
        in_specs=(
            P("alpha", "beta"),
            P("beta", None, None, None),
            P("alpha", None, None, None),
            P("beta", None),
            P("alpha", None),
            P("beta"),
            P("alpha"),
        ),
        out_specs=P("alpha", "beta"),
        check_vma=False,
    )
```

time: 70.2 us -> 70.3 us (level)
  no operation moved by 1% of the time
where the time goes in v2:
time: 70.3 us; the launch traced here: 70.2 us
  Pallas kernels  70.2 us (100%)
    pallas_call x1, Pallas kernels, on_device(): pl.pallas_call(functools.partial(kernel, na, nb), out_shape=pltpu.VMEM((S...  68.8 us
    pallas_call x1, Pallas kernels, on_device(): pl.pallas_call(store, out_shape=jax.ShapeDtypeStruct((S, S), jnp.float32)...  1.42 us

profile of v2, /device:TPU:2, one launch (start us, length us, event | category | flops | bytes accessed | tf_op | source)
XLA Modules:
  0.0 70.2 jit_solution(3668872552964581292)
XLA Ops:
  0.0 68.8 %sigma.1.total_ref = f32[768,768]{1,0:T(8,128)S(1)} custom-call(f32[768,768]{1,0:T(8,128)} %c_ref.1, f32[2,3,384,384]{3,2,1,0:T(8,128)} %hb_ref.1, f32[2,3,384,384]{3,2,1,0:T(8,128)} %ha_ref.1, s32[2,3]{1,0:T(2,128)} %lb_ref.1, s32[2,3]{1,0:T(2,128)} %la_ref.1, s32[2]{0:T(128)} %cb_ref.1, s32[2]{0:T(128)} %ca_ref.1), custom_call_target="tpu_custom_call" | custom-call | tf_op jit(solution)/shard_map/sigma/pallas_call | solution.py:355
  68.8 1.4 %store.1 = f32[768,768]{1,0:T(8,128)} custom-call(f32[768,768]{1,0:T(8,128)S(1)} %sigma.1.total_ref), custom_call_target="tpu_custom_call" | custom-call | tf_op jit(solution)/shard_map/store/pallas_call | solution.py:382

commit v3 on v2

--- a/solution.py
+++ b/solution.py
@@ -14,9 +14,11 @@
 S = G * GPD
 R = 64
 EVEN = 10
-LAST = 96
-CHUNKS = EVEN + 2
-FINAL = CHUNKS - 1
+REST = ((640, 32), (672, 64), (736, 32))
+CHUNKS = EVEN + len(REST)
+DETOUR = EVEN + 1
+STORES = 6
+TAIL = 128
 
 
 def split(x):
@@ -31,21 +33,25 @@
 
 def chunk(k):
     if isinstance(k, int) and k >= EVEN:
-        return pl.ds(*((EVEN * R, S - EVEN * R - LAST), (S - LAST, LAST))[k - EVEN])
+        return pl.ds(*REST[k - EVEN])
     return pl.ds(k * R, R)
 
 
 def kernel(
     na, nb,
-    c_ref, hb_ref, ha_ref, lb_ref, la_ref, cb_ref, ca_ref,
-    out_ref,
-    own, near, far, left, right, relay, detour, hb, ha,
+    c_ref, hb_ref, ha_ref, lb_in, la_in, cb_in, ca_in,
+    out_ref, wide_ref, stacked_ref,
+    lb_ref, la_ref, cb_ref, ca_ref, own, near, far, left, right, relay, detour, hb, ha,
     own_h, own_l, near_h, near_l, kb_h, kb_l, ka_h, ka_l,
     send_sem, recv_sem, near_sem, detour_sem, local_sem, ready_sem,
 ):
     a, b = lax.axis_index("alpha"), lax.axis_index("beta")
     nz = nb // 2
     core, z = lax.rem(a, 2), lax.rem(b, nz)
+
+    def turned(a):
+        return a + 2 - 4 * lax.rem(a // 2, 2)
+
     column = b - z
     low_wrap, high_wrap = z == 0, z == nz - 1
     wrap = jnp.logical_or(low_wrap, high_wrap)
@@ -55,15 +61,22 @@
     inner_device = (a, inner_b)
     outer_device = (far_a, inner_b)
     far_device = (far_a, b)
+    other_a = turned(a)
+    skip_device = (other_a, inner_b)
+    skipped_device = (lax.rem(other_a + 2 * core + na - 1, na), inner_b)
+    skipping_device = (turned(far_a), inner_b)
     up_device = (a, column + lax.rem(z + 1, nz))
     down_device = (a, column + lax.rem(z + nz - 1, nz))
 
-    own_copy = pltpu.make_async_copy(c_ref, own, local_sem.at[0])
-    hb_copy = pltpu.make_async_copy(hb_ref, hb, local_sem.at[1])
-    ha_copy = pltpu.make_async_copy(ha_ref, ha, local_sem.at[2])
-    own_copy.start()
-    hb_copy.start()
-    ha_copy.start()
+    loads = [
+        pltpu.make_async_copy(source, target, local_sem.at[i])
+        for i, (source, target) in enumerate(
+            (
+                (lb_in, lb_ref), (la_in, la_ref), (cb_in, cb_ref), (ca_in, ca_ref),
+                (hb_ref, hb), (ha_ref, ha), (c_ref, own),
+            )
+        )
+    ]
 
     def remote(source, target, flow, k, device):
         return pltpu.make_async_remote_copy(
@@ -94,23 +107,47 @@
         src_ref=c_ref, dst_ref=near, send_sem=near_sem.at[0], recv_sem=near_sem.at[1],
         device_id=core_device, device_id_type=MESH,
     )
-    to_detour = pltpu.make_async_remote_copy(
-        src_ref=c_ref.at[chunk(FINAL)], dst_ref=detour,
-        send_sem=send_sem.at[2, FINAL], recv_sem=detour_sem.at[0],
-        device_id=up_device, device_id_type=MESH,
-    )
-    from_detour = pltpu.make_async_remote_copy(
-        src_ref=detour, dst_ref=left.at[chunk(FINAL)],
-        send_sem=detour_sem.at[1], recv_sem=recv_sem.at[2, FINAL],
-        device_id=inner_device, device_id_type=MESH,
-    )
+
+    def held(k):
+        first, size = REST[k - EVEN]
+        return detour.at[pl.ds(first - REST[1][0], size)]
+
+    def to_detour(k):
+        return pltpu.make_async_remote_copy(
+            src_ref=c_ref.at[chunk(k)], dst_ref=held(k),
+            send_sem=send_sem.at[2, k], recv_sem=detour_sem.at[0, k - DETOUR],
+            device_id=up_device, device_id_type=MESH,
+        )
+
+    def from_detour(k):
+        return pltpu.make_async_remote_copy(
+            src_ref=held(k), dst_ref=left.at[chunk(k)],
+            send_sem=detour_sem.at[1, k - DETOUR], recv_sem=recv_sem.at[2, k],
+            device_id=inner_device, device_id_type=MESH,
+        )
+
+    def to_skip(k):
+        return pltpu.make_async_remote_copy(
+            src_ref=c_ref.at[chunk(k)], dst_ref=held(k),
+            send_sem=send_sem.at[1, k], recv_sem=detour_sem.at[0, k - DETOUR],
+            device_id=skip_device, device_id_type=MESH,
+        )
+
+    def from_skip(k):
+        return pltpu.make_async_remote_copy(
+            src_ref=held(k), dst_ref=far.at[chunk(k)],
+            send_sem=detour_sem.at[1, k - DETOUR], recv_sem=recv_sem.at[1, k],
+            device_id=skipped_device, device_id_type=MESH,
+        )
 
     def each(body, first=0, last=CHUNKS):
-        @pl.loop(first, min(last, EVEN))
-        def _(k):
-            body(k)
-
-        for k in range(EVEN, last):
+        if first < EVEN:
+
+            @pl.loop(first, min(last, EVEN))
+            def _(k):
+                body(k)
+
+        for k in range(max(first, EVEN), last):
             body(k)
 
     barrier = pltpu.get_barrier_semaphore()
@@ -122,7 +159,15 @@
         for device in (up_device, down_device):
             pl.semaphore_signal(barrier, inc=1, device_id=device, device_id_type=MESH)
 
-    pl.semaphore_wait(barrier, jnp.where(even, 4, 6))
+    @pl.when(high_wrap)
+    def _():
+        for device in (skip_device, skipped_device, skipping_device):
+            pl.semaphore_signal(barrier, inc=1, device_id=device, device_id_type=MESH)
+
+    for load in loads:
+        load.start()
+
+    pl.semaphore_wait(barrier, jnp.where(even, 4, jnp.where(high_wrap, 9, 6)))
 
     @pl.when(jnp.logical_not(even))
     def _():
@@ -131,37 +176,37 @@
 
     @pl.when(wrap)
     def _():
-        each(lambda k: to_inner(k).start(), last=FINAL)
+        each(lambda k: to_inner(k).start(), last=DETOUR)
 
     @pl.when(low_wrap)
     def _():
-        to_inner(FINAL).start()
+        each(lambda k: to_inner(k).start(), first=DETOUR)
 
     @pl.when(jnp.logical_not(wrap))
     def _():
-        each(lambda k: to_far(k).start(), last=FINAL)
+        each(lambda k: to_far(k).start())
+
+    @pl.when(high_wrap)
+    def _():
+        each(lambda k: to_skip(k).start(), first=DETOUR)
+
+    to_core.start()
+
+    @pl.when(even)
+    def _():
+        pl.semaphore_wait(ready_sem, 2)
+
+    @pl.when(high_wrap)
+    def _():
+        each(lambda k: to_detour(k).start(), first=DETOUR)
+
+    @pl.when(jnp.logical_not(high_wrap))
+    def _():
+        each(lambda k: to_up(k).start())
 
     @pl.when(jnp.logical_not(low_wrap))
     def _():
-        to_far(FINAL).start()
-
-    @pl.when(even)
-    def _():
-        pl.semaphore_wait(ready_sem, 2)
-
-    @pl.when(high_wrap)
-    def _():
-        to_detour.start()
-
-    @pl.when(jnp.logical_not(high_wrap))
-    def _():
-        each(lambda k: to_up(k).start())
-
-    @pl.when(jnp.logical_not(low_wrap))
-    def _():
         each(lambda k: to_down(k).start())
-
-    to_core.start()
 
     def forward(k):
         @pl.when(wrap)
@@ -179,6 +224,13 @@
         @pl.when(wrap)
         def _():
             to_outer(k).start()
+
+    near_at = jnp.where(core == 1, 0, 2 * S)
+    far_at = 2 * S - near_at
+    mine = pl.ds(S, S)
+
+    def third(i):
+        return pl.ds(pl.multiple_of(i * 256, 256), 256)
 
     def select(blocks, links, counts, t, group, rows):
         total = None
@@ -208,12 +260,7 @@
         own_h[rows, :], own_l[rows, :] = split(own[rows, :])
 
     def arrived(copy, first, last):
-        @pl.loop(first, min(last, EVEN))
-        def _(k):
-            copy(k).wait_recv()
-
-        for k in range(max(first, EVEN), last):
-            copy(k).wait_recv()
+        each(lambda k: copy(k).wait_recv(), first, last)
 
     def side(block, at, first, size):
         rows, theirs = pl.ds(first, size), pl.ds(at, S)
@@ -224,28 +271,26 @@
             arrived(copy, first // R, (first + size) // R)
             side(block, at, first, size)
 
+    def stack(first, size):
+        high, low = split(far[pl.ds(first, size), :])
+        return jnp.concatenate([high, high, low], axis=0)
+
+    def widen(block, first, size):
+        theirs = pl.ds(pl.multiple_of(far_at + first, 128), size)
+        high, low = ka_h[block, theirs], ka_l[block, theirs]
+        return jnp.concatenate([high, low, high], axis=1)
+
     def outer(first, size):
-        theirs = pl.ds(pl.multiple_of(far_at + first, 128), size)
-        high, low = split(far[pl.ds(first, size), :])
-        stacked = jnp.concatenate([high, high, low], axis=0)
+        stacked = stack(first, size)
 
         @pl.loop(0, 3)
         def _(i):
-            block = pl.ds(pl.multiple_of(i * 256, 256), 256)
-            high, low = ka_h[block, theirs], ka_l[block, theirs]
-            wide = jnp.concatenate([high, low, high], axis=1)
+            block = third(i)
+            wide = widen(block, first, size)
             out_ref[block, :] += jnp.dot(wide, stacked, preferred_element_type=jnp.float32)
 
-    near_at = jnp.where(core == 1, 0, 2 * S)
-    far_at = 2 * S - near_at
-    mine = pl.ds(S, S)
-
-    def third(i):
-        return pl.ds(pl.multiple_of(i * 256, 256), 256)
-
-    own_copy.wait()
-    hb_copy.wait()
-    ha_copy.wait()
+    for load in loads:
+        load.wait()
 
     @pl.loop(0, 2)
     def _(step):
@@ -274,13 +319,21 @@
 
     @pl.when(low_wrap)
     def _():
-        to_detour.wait_recv()
-        from_detour.start()
+        for k in range(DETOUR, CHUNKS):
+            to_detour(k).wait_recv()
+            from_detour(k).start()
+
+    @pl.when(high_wrap)
+    def _():
+        for k in range(DETOUR, CHUNKS):
+            to_skip(k).wait_recv()
+            from_skip(k).start()
 
     @pl.loop(0, 3)
     def _(i):
         rows = third(i)
         near_h[rows, :], near_l[rows, :] = split(near[rows, :])
+        wide_ref[rows, :] = widen(rows, S - TAIL, TAIL)
 
     forward(5)
 
@@ -306,7 +359,8 @@
 
     @pl.when(low_wrap)
     def _():
-        forward(FINAL)
+        for k in range(DETOUR, CHUNKS):
+            forward(k)
 
     sides(512, 128)
     arrived(to_far, 8, 10)
@@ -316,29 +370,43 @@
 
     @pl.when(wrap)
     def _():
-        each(lambda k: to_inner(k).wait_send(), last=FINAL)
+        each(lambda k: to_inner(k).wait_send(), last=DETOUR)
 
     @pl.when(low_wrap)
     def _():
-        to_inner(FINAL).wait_send()
-        from_detour.wait_send()
+        for k in range(DETOUR, CHUNKS):
+            to_inner(k).wait_send()
+            from_detour(k).wait_send()
+
+    @pl.when(high_wrap)
+    def _():
+        for k in range(DETOUR, CHUNKS):
+            from_skip(k).wait_send()
 
     arrived(to_down, EVEN, CHUNKS)
     side(right, 2 * S, 640, 128)
     arrived(to_up, EVEN, CHUNKS)
     side(left, 0, 640, 128)
     arrived(to_far, EVEN, CHUNKS)
-    outer(640, 128)
+    stacked_ref[...] = stack(S - TAIL, TAIL)
 
     each(lambda k: to_far(k).wait_send())
     each(lambda k: to_up(k).wait_send())
     each(lambda k: to_down(k).wait_send())
 
 
-def store(total_ref, out_ref, sem):
-    copy = pltpu.make_async_copy(total_ref, out_ref, sem)
-    copy.start()
-    copy.wait()
+def store(total_ref, wide_ref, stacked_ref, out_ref, result, sem):
+    size = S // STORES
+    copies = []
+    for i in range(STORES):
+        rows = pl.ds(i * size, size)
+        result[rows, :] = total_ref[rows, :] + jnp.dot(
+            wide_ref[rows, :], stacked_ref[...], preferred_element_type=jnp.float32
+        )
+        copies.append(pltpu.make_async_copy(result.at[rows], out_ref.at[rows], sem.at[i]))
+        copies[-1].start()
+    for copy in copies:
+        copy.wait()
 
 
 def solution(mesh):
@@ -352,14 +420,19 @@
         half = pltpu.VMEM((S, S), jnp.bfloat16)
         tall = pltpu.VMEM((3 * S, S), jnp.bfloat16)
         wide = pltpu.VMEM((S, 3 * S), jnp.bfloat16)
-        total = pl.pallas_call(
+        total, wide_rows, stacked = pl.pallas_call(
             functools.partial(kernel, na, nb),
-            out_shape=pltpu.VMEM((S, S), jnp.float32),
-            in_specs=[pl.BlockSpec(memory_space=pltpu.HBM)] * 3
-            + [pl.BlockSpec(memory_space=pltpu.SMEM)] * 4,
-            out_specs=pl.BlockSpec(memory_space=pltpu.VMEM),
-            scratch_shapes=[block] * 6
-            + [pltpu.VMEM((LAST, S), jnp.float32)]
+            out_shape=(
+                pltpu.VMEM((S, S), jnp.float32),
+                pltpu.VMEM((S, 3 * TAIL), jnp.bfloat16),
+                pltpu.VMEM((3 * TAIL, S), jnp.bfloat16),
+            ),
+            in_specs=[pl.BlockSpec(memory_space=pltpu.HBM)] * 7,
+            out_specs=[pl.BlockSpec(memory_space=pltpu.VMEM)] * 3,
+            scratch_shapes=[pltpu.SMEM((GPD, LIST), jnp.int32)] * 2
+            + [pltpu.SMEM((GPD,), jnp.int32)] * 2
+            + [block] * 6
+            + [pltpu.VMEM((S - REST[1][0], S), jnp.float32)]
             + [listed] * 2
             + [half] * 4
             + [tall, tall, wide, wide]
@@ -367,8 +440,8 @@
                 pltpu.SemaphoreType.DMA((4, CHUNKS)),
                 pltpu.SemaphoreType.DMA((4, CHUNKS)),
                 pltpu.SemaphoreType.DMA((2,)),
-                pltpu.SemaphoreType.DMA((2,)),
-                pltpu.SemaphoreType.DMA((3,)),
+                pltpu.SemaphoreType.DMA((2, 2)),
+                pltpu.SemaphoreType.DMA((7,)),
                 pltpu.SemaphoreType.REGULAR,
             ],
             compiler_params=pltpu.CompilerParams(
@@ -382,12 +455,12 @@
         return pl.pallas_call(
             store,
             out_shape=jax.ShapeDtypeStruct((S, S), jnp.float32),
-            in_specs=[pl.BlockSpec(memory_space=pltpu.VMEM)],
+            in_specs=[pl.BlockSpec(memory_space=pltpu.VMEM)] * 3,
             out_specs=pl.BlockSpec(memory_space=pl.ANY),
-            scratch_shapes=[pltpu.SemaphoreType.DMA],
+            scratch_shapes=[block, pltpu.SemaphoreType.DMA((STORES,))],
             compiler_params=pltpu.CompilerParams(vmem_limit_bytes=8 * 2**20),
             name="store",
-        )(total)
+        )(total, wide_rows, stacked)
 
     return jax.shard_map(
         on_device,

time: 70.3 us -> 66.8 us (0.950)
  Pallas kernels: 70.2 us -> 66.7 us
    pallas_call x1, Pallas kernels: 68.8 us -> 65 us  [on_device(): pl.pallas_call(functools.partial(kernel, na, nb), out_shape=(pltpu.VMEM((...]
where the time goes in v3:
time: 66.8 us; the launch traced here: 66.7 us
  Pallas kernels  66.7 us (100%)
    pallas_call x1, Pallas kernels, on_device(): pl.pallas_call(functools.partial(kernel, na, nb), out_shape=(pltpu.VMEM((...  65 us
    pallas_call x1, Pallas kernels, on_device(): pl.pallas_call(store, out_shape=jax.ShapeDtypeStruct((S, S), jnp.float32)...  1.75 us

profile of v3, /device:TPU:2, one launch (start us, length us, event | category | flops | bytes accessed | tf_op | source)
XLA Modules:
  0.0 66.7 jit_solution(12845542946748777414)
XLA Ops:
  0.0 65.0 %sigma.1 = (f32[768,768]{1,0:T(8,128)S(1)}, bf16[768,384]{1,0:T(8,128)(2,1)S(1)}, bf16[384,768]{1,0:T(8,128)(2,1)S(1)}) custom-call(f32[768,768]{1,0:T(8,128)} %c_ref.1, f32[2,3,384,384]{3,2,1,0:T(8,128)} %hb_ref.1, f32[2,3,384,384]{3,2,1,0:T(8,128)} %ha_ref.1, s32[2,3]{1,0:T(2,128)} %lb_in.1, s32[2,3]{1,0:T(2,128)} %la_in.1, s32[2]{0:T(128)} %cb_in.1, s32[2]{0:T(128)} %ca_in.1), custom_call_target="tpu_custom_call" | custom-call | tf_op jit(solution)/shard_map/sigma/pallas_call | solution.py:423
  65.0 1.7 %store.1 = f32[768,768]{1,0:T(8,128)} custom-call(f32[768,768]{1,0:T(8,128)S(1)} %get-tuple-element.8.total_ref, bf16[768,384]{1,0:T(8,128)(2,1)S(1)} %get-tuple-element.9.wide_ref, bf16[384,768]{1,0:T(8,128)(2,1)S(1)} %get-tuple-element.10.stacked_ref), custom_call_target="tpu_custom_call" | custom-call | tf_op jit(solution)/shard_map/store/pallas_call | solution.py:455

commit v4 on v3

--- a/solution.py
+++ b/solution.py
@@ -17,8 +17,11 @@
 REST = ((640, 32), (672, 64), (736, 32))
 CHUNKS = EVEN + len(REST)
 DETOUR = EVEN + 1
+LAST = S - REST[1][0]
+FAR = ((0, 256), (256, 256), (512, 128), (640, 128))
 STORES = 6
 TAIL = 128
+SIDES = S // TAIL
 
 
 def split(x):
@@ -43,7 +46,7 @@
     out_ref, wide_ref, stacked_ref,
     lb_ref, la_ref, cb_ref, ca_ref, own, near, far, left, right, relay, detour, hb, ha,
     own_h, own_l, near_h, near_l, kb_h, kb_l, ka_h, ka_l,
-    send_sem, recv_sem, near_sem, detour_sem, local_sem, ready_sem,
+    send_sem, relay_sem, far_sem, left_sem, right_sem, near_sem, detour_sem, local_sem, ready_sem,
 ):
     a, b = lax.axis_index("alpha"), lax.axis_index("beta")
     nz = nb // 2
@@ -78,96 +81,66 @@
         )
     ]
 
-    def remote(source, target, flow, k, device):
+    whole, most, last = pl.ds(0, S), pl.ds(0, S - LAST), pl.ds(S - LAST, LAST)
+
+    def remote(source, target, send, recv, device):
         return pltpu.make_async_remote_copy(
-            src_ref=source.at[chunk(k)],
-            dst_ref=target.at[chunk(k)],
-            send_sem=send_sem.at[flow, k],
-            recv_sem=recv_sem.at[flow, k],
-            device_id=device,
-            device_id_type=MESH,
+            src_ref=source, dst_ref=target, send_sem=send, recv_sem=recv,
+            device_id=device, device_id_type=MESH,
         )
 
-    def to_inner(k):
-        return remote(c_ref, relay, 0, k, inner_device)
-
-    def to_far(k):
-        return remote(c_ref, far, 1, k, far_device)
-
-    def to_outer(k):
-        return remote(relay, far, 1, k, outer_device)
-
-    def to_up(k, source=c_ref):
-        return remote(source, left, 2, k, up_device)
-
-    def to_down(k, source=c_ref):
-        return remote(source, right, 3, k, down_device)
-
-    to_core = pltpu.make_async_remote_copy(
-        src_ref=c_ref, dst_ref=near, send_sem=near_sem.at[0], recv_sem=near_sem.at[1],
-        device_id=core_device, device_id_type=MESH,
+    def to_inner(rows, k):
+        source, target = c_ref.at[rows], relay.at[rows]
+        return remote(source, target, send_sem.at[0], relay_sem.at[k], inner_device)
+
+    def to_far(rows, at, source=c_ref, device=far_device):
+        return remote(source.at[rows], far.at[rows], send_sem.at[1], far_sem.at[at], device)
+
+    def to_up(rows, at, source=c_ref):
+        return remote(source.at[rows], left.at[rows], send_sem.at[2], left_sem.at[at], up_device)
+
+    def to_down(rows, at, source=c_ref):
+        source, target = source.at[rows], right.at[rows]
+        return remote(source, target, send_sem.at[3], right_sem.at[at], down_device)
+
+    to_core = remote(c_ref, near, near_sem.at[0], near_sem.at[1], core_device)
+    mine_last = c_ref.at[last]
+    to_detour = remote(mine_last, detour, send_sem.at[2], detour_sem.at[0], up_device)
+    to_skip = remote(mine_last, detour, send_sem.at[1], detour_sem.at[0], skip_device)
+    from_detour = remote(
+        detour, left.at[last], detour_sem.at[1], left_sem.at[SIDES - 1], inner_device
     )
-
-    def held(k):
-        first, size = REST[k - EVEN]
-        return detour.at[pl.ds(first - REST[1][0], size)]
-
-    def to_detour(k):
-        return pltpu.make_async_remote_copy(
-            src_ref=c_ref.at[chunk(k)], dst_ref=held(k),
-            send_sem=send_sem.at[2, k], recv_sem=detour_sem.at[0, k - DETOUR],
-            device_id=up_device, device_id_type=MESH,
-        )
-
-    def from_detour(k):
-        return pltpu.make_async_remote_copy(
-            src_ref=held(k), dst_ref=left.at[chunk(k)],
-            send_sem=detour_sem.at[1, k - DETOUR], recv_sem=recv_sem.at[2, k],
-            device_id=inner_device, device_id_type=MESH,
-        )
-
-    def to_skip(k):
-        return pltpu.make_async_remote_copy(
-            src_ref=c_ref.at[chunk(k)], dst_ref=held(k),
-            send_sem=send_sem.at[1, k], recv_sem=detour_sem.at[0, k - DETOUR],
-            device_id=skip_device, device_id_type=MESH,
-        )
-
-    def from_skip(k):
-        return pltpu.make_async_remote_copy(
-            src_ref=held(k), dst_ref=far.at[chunk(k)],
-            send_sem=detour_sem.at[1, k - DETOUR], recv_sem=recv_sem.at[1, k],
-            device_id=skipped_device, device_id_type=MESH,
-        )
-
-    def each(body, first=0, last=CHUNKS):
-        if first < EVEN:
-
-            @pl.loop(first, min(last, EVEN))
-            def _(k):
-                body(k)
-
-        for k in range(max(first, EVEN), last):
+    from_skip = remote(
+        detour, far.at[last], detour_sem.at[1], far_sem.at[len(FAR) - 1], skipped_device
+    )
+
+    def each(body, chunks):
+        @pl.loop(0, EVEN)
+        def _(k):
             body(k)
 
+        for k in range(EVEN, chunks):
+            body(k)
+
+    def side_rows(p):
+        return pl.ds(pl.multiple_of(p * TAIL, TAIL), TAIL)
+
     barrier = pltpu.get_barrier_semaphore()
-    for device in (core_device, inner_device, outer_device, far_device):
-        pl.semaphore_signal(barrier, inc=1, device_id=device, device_id_type=MESH)
-
-    @pl.when(even)
-    def _():
-        for device in (up_device, down_device):
+
+    def greet(*devices):
+        for device in devices:
             pl.semaphore_signal(barrier, inc=1, device_id=device, device_id_type=MESH)
 
-    @pl.when(high_wrap)
-    def _():
-        for device in (skip_device, skipped_device, skipping_device):
-            pl.semaphore_signal(barrier, inc=1, device_id=device, device_id_type=MESH)
+    greet(core_device)
+    pl.when(wrap)(lambda: greet(inner_device, outer_device))
+    pl.when(jnp.logical_not(wrap))(lambda: greet(far_device))
+    pl.when(even)(lambda: greet(up_device, down_device))
+    pl.when(high_wrap)(lambda: greet(skip_device, skipped_device, skipping_device))
 
     for load in loads:
         load.start()
 
-    pl.semaphore_wait(barrier, jnp.where(even, 4, jnp.where(high_wrap, 9, 6)))
+    pl.semaphore_wait(barrier, jnp.where(wrap, 3, 2) + jnp.where(even, 0, 2) + jnp.where(high_wrap, 3, 0))
 
     @pl.when(jnp.logical_not(even))
     def _():
@@ -176,21 +149,21 @@
 
     @pl.when(wrap)
     def _():
-        each(lambda k: to_inner(k).start(), last=DETOUR)
+        each(lambda k: to_inner(chunk(k), k).start(), DETOUR)
 
     @pl.when(low_wrap)
     def _():
-        each(lambda k: to_inner(k).start(), first=DETOUR)
+        for k in range(DETOUR, CHUNKS):
+            to_inner(chunk(k), k).start()
 
     @pl.when(jnp.logical_not(wrap))
     def _():
-        each(lambda k: to_far(k).start())
+        for at, rows in enumerate(FAR):
+            to_far(pl.ds(*rows), at).start()
 
     @pl.when(high_wrap)
     def _():
-        each(lambda k: to_skip(k).start(), first=DETOUR)
-
-    to_core.start()
+        to_skip.start()
 
     @pl.when(even)
     def _():
@@ -198,32 +171,41 @@
 
     @pl.when(high_wrap)
     def _():
-        each(lambda k: to_detour(k).start(), first=DETOUR)
+        to_detour.start()
 
     @pl.when(jnp.logical_not(high_wrap))
     def _():
-        each(lambda k: to_up(k).start())
+        @pl.loop(0, SIDES)
+        def _(p):
+            to_up(side_rows(p), p).start()
 
     @pl.when(jnp.logical_not(low_wrap))
     def _():
-        each(lambda k: to_down(k).start())
+        @pl.loop(0, SIDES)
+        def _(p):
+            to_down(side_rows(p), p).start()
 
     def forward(k):
+        rows = chunk(k)
+        rest = isinstance(k, int) and k >= EVEN
+        side_at, far_block = (SIDES - 1, len(FAR) - 1) if rest else (k // 2, k // 4)
+
         @pl.when(wrap)
         def _():
-            to_inner(k).wait_recv()
+            to_inner(rows, k).wait_recv()
 
         @pl.when(high_wrap)
         def _():
-            to_up(k, relay).start()
+            to_up(rows, side_at, relay).start()
 
         @pl.when(low_wrap)
         def _():
-            to_down(k, relay).start()
+            to_down(rows, side_at, relay).start()
 
         @pl.when(wrap)
         def _():
-            to_outer(k).start()
+            to_outer = to_far(rows, far_block, relay, outer_device)
+            to_outer.start()
 
     near_at = jnp.where(core == 1, 0, 2 * S)
     far_at = 2 * S - near_at
@@ -259,19 +241,18 @@
         rows = pl.ds(pl.multiple_of(s * 128, 128), 128)
         own_h[rows, :], own_l[rows, :] = split(own[rows, :])
 
-    def arrived(copy, first, last):
-        each(lambda k: copy(k).wait_recv(), first, last)
-
-    def side(block, at, first, size):
-        rows, theirs = pl.ds(first, size), pl.ds(at, S)
+    def side(copy, block, at, p):
+        rows, theirs = side_rows(p), pl.ds(at, S)
+        copy(rows, p).wait_recv()
         out_ref[rows, :] += product(*split(block[rows, :]), kb_h[theirs, :], kb_l[theirs, :])
 
-    def sides(first, size):
-        for copy, block, at in ((to_up, left, 0), (to_down, right, 2 * S)):
-            arrived(copy, first // R, (first + size) // R)
-            side(block, at, first, size)
-
-    def stack(first, size):
+    def sides(p):
+        side(to_down, right, 2 * S, p)
+        side(to_up, left, 0, p)
+
+    def stack(at):
+        first, size = FAR[at]
+        to_far(pl.ds(first, size), at).wait_recv()
         high, low = split(far[pl.ds(first, size), :])
         return jnp.concatenate([high, high, low], axis=0)
 
@@ -280,8 +261,9 @@
         high, low = ka_h[block, theirs], ka_l[block, theirs]
         return jnp.concatenate([high, low, high], axis=1)
 
-    def outer(first, size):
-        stacked = stack(first, size)
+    def outer(at):
+        first, size = FAR[at]
+        stacked = stack(at)
 
         @pl.loop(0, 3)
         def _(i):
@@ -301,6 +283,7 @@
             build(3 * step + i)
 
     forward(2)
+    to_core.start()
 
     @pl.loop(0, 3)
     def _(i):
@@ -319,15 +302,13 @@
 
     @pl.when(low_wrap)
     def _():
-        for k in range(DETOUR, CHUNKS):
-            to_detour(k).wait_recv()
-            from_detour(k).start()
+        to_detour.wait_recv()
+        from_detour.start()
 
     @pl.when(high_wrap)
     def _():
-        for k in range(DETOUR, CHUNKS):
-            to_skip(k).wait_recv()
-            from_skip(k).start()
+        to_skip.wait_recv()
+        from_skip.start()
 
     @pl.loop(0, 3)
     def _(i):
@@ -344,55 +325,47 @@
         out_ref[rows, :] += product(ka_h[rows, theirs], ka_l[rows, theirs], near_h[...], near_l[...])
 
     forward(6)
-    sides(0, 128)
+    sides(0)
     forward(7)
-    sides(128, 128)
+    sides(1)
     forward(8)
-    arrived(to_far, 0, 4)
-    outer(0, 256)
+    outer(0)
     forward(9)
-    sides(256, 128)
-    forward(10)
-    arrived(to_far, 4, 8)
-    outer(256, 256)
-    sides(384, 128)
+    sides(2)
+    forward(EVEN)
+    outer(1)
 
     @pl.when(low_wrap)
     def _():
-        for k in range(DETOUR, CHUNKS):
-            forward(k)
-
-    sides(512, 128)
-    arrived(to_far, 8, 10)
-    outer(512, 128)
-
+        forward(DETOUR)
+
+    sides(3)
+
+    @pl.when(low_wrap)
+    def _():
+        forward(DETOUR + 1)
+
+    sides(4)
+    outer(2)
     to_core.wait_send()
+    sides(SIDES - 1)
+    stacked_ref[...] = stack(len(FAR) - 1)
+
+    @pl.when(high_wrap)
+    def _():
+        to_inner(most, 0).wait_send()
+
+    @pl.when(low_wrap)
+    def _():
+        to_inner(whole, 0).wait_send()
 
     @pl.when(wrap)
     def _():
-        each(lambda k: to_inner(k).wait_send(), last=DETOUR)
-
-    @pl.when(low_wrap)
-    def _():
-        for k in range(DETOUR, CHUNKS):
-            to_inner(k).wait_send()
-            from_detour(k).wait_send()
-
-    @pl.when(high_wrap)
-    def _():
-        for k in range(DETOUR, CHUNKS):
-            from_skip(k).wait_send()
-
-    arrived(to_down, EVEN, CHUNKS)
-    side(right, 2 * S, 640, 128)
-    arrived(to_up, EVEN, CHUNKS)
-    side(left, 0, 640, 128)
-    arrived(to_far, EVEN, CHUNKS)
-    stacked_ref[...] = stack(S - TAIL, TAIL)
-
-    each(lambda k: to_far(k).wait_send())
-    each(lambda k: to_up(k).wait_send())
-    each(lambda k: to_down(k).wait_send())
+        from_detour.wait_send()
+
+    to_far(whole, 0).wait_send()
+    to_up(whole, 0).wait_send()
+    to_down(whole, 0).wait_send()
 
 
 def store(total_ref, wide_ref, stacked_ref, out_ref, result, sem):
@@ -432,15 +405,18 @@
             scratch_shapes=[pltpu.SMEM((GPD, LIST), jnp.int32)] * 2
             + [pltpu.SMEM((GPD,), jnp.int32)] * 2
             + [block] * 6
-            + [pltpu.VMEM((S - REST[1][0], S), jnp.float32)]
+            + [pltpu.VMEM((LAST, S), jnp.float32)]
             + [listed] * 2
             + [half] * 4
             + [tall, tall, wide, wide]
             + [
-                pltpu.SemaphoreType.DMA((4, CHUNKS)),
-                pltpu.SemaphoreType.DMA((4, CHUNKS)),
+                pltpu.SemaphoreType.DMA((4,)),
+                pltpu.SemaphoreType.DMA((CHUNKS,)),
+                pltpu.SemaphoreType.DMA((len(FAR),)),
+                pltpu.SemaphoreType.DMA((SIDES,)),
+                pltpu.SemaphoreType.DMA((SIDES,)),
                 pltpu.SemaphoreType.DMA((2,)),
-                pltpu.SemaphoreType.DMA((2, 2)),
+                pltpu.SemaphoreType.DMA((2,)),
                 pltpu.SemaphoreType.DMA((7,)),
                 pltpu.SemaphoreType.REGULAR,
             ],

time: 66.8 us -> 65.9 us (0.987)
  Pallas kernels: 66.7 us -> 65.8 us
    pallas_call x1, Pallas kernels: 65 us -> 64.1 us  [on_device(): pl.pallas_call(functools.partial(kernel, na, nb), out_shape=(pltpu.VMEM((...]
where the time goes in v4:
time: 65.9 us; the launch traced here: 65.8 us
  Pallas kernels  65.8 us (100%)
    pallas_call x1, Pallas kernels, on_device(): pl.pallas_call(functools.partial(kernel, na, nb), out_shape=(pltpu.VMEM((...  64.1 us
    pallas_call x1, Pallas kernels, on_device(): pl.pallas_call(store, out_shape=jax.ShapeDtypeStruct((S, S), jnp.float32)...  1.75 us

profile of v4, /device:TPU:2, one launch (start us, length us, event | category | flops | bytes accessed | tf_op | source)
XLA Modules:
  0.0 65.8 jit_solution(16788213408001052340)
XLA Ops:
  0.0 64.1 %sigma.1 = (f32[768,768]{1,0:T(8,128)S(1)}, bf16[768,384]{1,0:T(8,128)(2,1)S(1)}, bf16[384,768]{1,0:T(8,128)(2,1)S(1)}) custom-call(f32[768,768]{1,0:T(8,128)} %c_ref.1, f32[2,3,384,384]{3,2,1,0:T(8,128)} %hb_ref.1, f32[2,3,384,384]{3,2,1,0:T(8,128)} %ha_ref.1, s32[2,3]{1,0:T(2,128)} %lb_in.1, s32[2,3]{1,0:T(2,128)} %la_in.1, s32[2]{0:T(128)} %cb_in.1, s32[2]{0:T(128)} %ca_in.1), custom_call_target="tpu_custom_call" | custom-call | tf_op jit(solution)/shard_map/sigma/pallas_call | solution.py:396
  64.1 1.7 %store.1 = f32[768,768]{1,0:T(8,128)} custom-call(f32[768,768]{1,0:T(8,128)S(1)} %get-tuple-element.8.total_ref, bf16[768,384]{1,0:T(8,128)(2,1)S(1)} %get-tuple-element.9.wide_ref, bf16[384,768]{1,0:T(8,128)(2,1)S(1)} %get-tuple-element.10.stacked_ref), custom_call_target="tpu_custom_call" | custom-call | tf_op jit(solution)/shard_map/store/pallas_call | solution.py:431

commit v5 on v4

--- a/solution.py
+++ b/solution.py
@@ -14,7 +14,7 @@
 S = G * GPD
 R = 64
 EVEN = 10
-REST = ((640, 32), (672, 64), (736, 32))
+REST = ((640, 48), (688, 48), (736, 32))
 CHUNKS = EVEN + len(REST)
 DETOUR = EVEN + 1
 LAST = S - REST[1][0]
@@ -147,6 +147,10 @@
         for device in (up_device, down_device):
             pl.semaphore_signal(ready_sem, inc=1, device_id=device, device_id_type=MESH)
 
+    @pl.when(high_wrap)
+    def _():
+        to_detour.start()
+
     @pl.when(wrap)
     def _():
         each(lambda k: to_inner(chunk(k), k).start(), DETOUR)
@@ -169,21 +173,17 @@
     def _():
         pl.semaphore_wait(ready_sem, 2)
 
-    @pl.when(high_wrap)
-    def _():
-        to_detour.start()
+    @pl.when(jnp.logical_not(low_wrap))
+    def _():
+        @pl.loop(0, SIDES)
+        def _(p):
+            to_down(side_rows(p), p).start()
 
     @pl.when(jnp.logical_not(high_wrap))
     def _():
         @pl.loop(0, SIDES)
         def _(p):
             to_up(side_rows(p), p).start()
-
-    @pl.when(jnp.logical_not(low_wrap))
-    def _():
-        @pl.loop(0, SIDES)
-        def _(p):
-            to_down(side_rows(p), p).start()
 
     def forward(k):
         rows = chunk(k)

time: 65.9 us -> 65.9 us (level)
  no operation moved by 1% of the time
where the time goes in v5:
time: 65.9 us; the launch traced here: 65.8 us
  Pallas kernels  65.8 us (100%)
    pallas_call x1, Pallas kernels, on_device(): pl.pallas_call(functools.partial(kernel, na, nb), out_shape=(pltpu.VMEM((...  64.1 us
    pallas_call x1, Pallas kernels, on_device(): pl.pallas_call(store, out_shape=jax.ShapeDtypeStruct((S, S), jnp.float32)...  1.75 us

profile of v5, /device:TPU:2, one launch (start us, length us, event | category | flops | bytes accessed | tf_op | source)
XLA Modules:
  0.0 65.8 jit_solution(3749774567746415010)
XLA Ops:
  0.0 64.1 %sigma.1 = (f32[768,768]{1,0:T(8,128)S(1)}, bf16[768,384]{1,0:T(8,128)(2,1)S(1)}, bf16[384,768]{1,0:T(8,128)(2,1)S(1)}) custom-call(f32[768,768]{1,0:T(8,128)} %c_ref.1, f32[2,3,384,384]{3,2,1,0:T(8,128)} %hb_ref.1, f32[2,3,384,384]{3,2,1,0:T(8,128)} %ha_ref.1, s32[2,3]{1,0:T(2,128)} %lb_in.1, s32[2,3]{1,0:T(2,128)} %la_in.1, s32[2]{0:T(128)} %cb_in.1, s32[2]{0:T(128)} %ca_in.1), custom_call_target="tpu_custom_call" | custom-call | tf_op jit(solution)/shard_map/sigma/pallas_call | solution.py:396
  64.1 1.7 %store.1 = f32[768,768]{1,0:T(8,128)} custom-call(f32[768,768]{1,0:T(8,128)S(1)} %get-tuple-element.8.total_ref, bf16[768,384]{1,0:T(8,128)(2,1)S(1)} %get-tuple-element.9.wide_ref, bf16[384,768]{1,0:T(8,128)(2,1)S(1)} %get-tuple-element.10.stacked_ref), custom_call_target="tpu_custom_call" | custom-call | tf_op jit(solution)/shard_map/store/pallas_call | solution.py:431

commit v6 on v5

--- a/solution.py
+++ b/solution.py
@@ -14,7 +14,7 @@
 S = G * GPD
 R = 64
 EVEN = 10
-REST = ((640, 48), (688, 48), (736, 32))
+REST = ((640, 32), (672, 64), (736, 32))
 CHUNKS = EVEN + len(REST)
 DETOUR = EVEN + 1
 LAST = S - REST[1][0]

time: 65.9 us -> 65.9 us (level)
  no operation moved by 1% of the time
where the time goes in v6:
time: 65.9 us; the launch traced here: 65.8 us
  Pallas kernels  65.8 us (100%)
    pallas_call x1, Pallas kernels, on_device(): pl.pallas_call(functools.partial(kernel, na, nb), out_shape=(pltpu.VMEM((...  64.1 us
    pallas_call x1, Pallas kernels, on_device(): pl.pallas_call(store, out_shape=jax.ShapeDtypeStruct((S, S), jnp.float32)...  1.75 us

profile of v6, /device:TPU:2, one launch (start us, length us, event | category | flops | bytes accessed | tf_op | source)
XLA Modules:
  0.0 65.8 jit_solution(15037539498128258505)
XLA Ops:
  0.0 64.1 %sigma.1 = (f32[768,768]{1,0:T(8,128)S(1)}, bf16[768,384]{1,0:T(8,128)(2,1)S(1)}, bf16[384,768]{1,0:T(8,128)(2,1)S(1)}) custom-call(f32[768,768]{1,0:T(8,128)} %c_ref.1, f32[2,3,384,384]{3,2,1,0:T(8,128)} %hb_ref.1, f32[2,3,384,384]{3,2,1,0:T(8,128)} %ha_ref.1, s32[2,3]{1,0:T(2,128)} %lb_in.1, s32[2,3]{1,0:T(2,128)} %la_in.1, s32[2]{0:T(128)} %cb_in.1, s32[2]{0:T(128)} %ca_in.1), custom_call_target="tpu_custom_call" | custom-call | tf_op jit(solution)/shard_map/sigma/pallas_call | solution.py:396
  64.1 1.7 %store.1 = f32[768,768]{1,0:T(8,128)} custom-call(f32[768,768]{1,0:T(8,128)S(1)} %get-tuple-element.8.total_ref, bf16[768,384]{1,0:T(8,128)(2,1)S(1)} %get-tuple-element.9.wide_ref, bf16[384,768]{1,0:T(8,128)(2,1)S(1)} %get-tuple-element.10.stacked_ref), custom_call_target="tpu_custom_call" | custom-call | tf_op jit(solution)/shard_map/store/pallas_call | solution.py:431
